TPU v7x, 32 devices: a whole 2x2x4 slice. The times are simulated.
32 devices in a mesh: parts: 2 (over y), vocab: 4 (over z), mp: 2 (over x), rep: 2 (over core).
Axes of the slice: x: 2, y: 2, z: 4, core: 2. Of those that a mesh axis runs over, the one named last changes fastest.
Arguments:
- resid_base: bfloat16 [128, 4608], P(('parts', 'vocab', 'rep'), 'mp'), parts along dimension 0, may hold values from -60 to 60
- mlp_hidden: bfloat16 [128, 36864], P(('parts', 'vocab', 'rep'), 'mp'), parts along dimension 0, may hold values from -6 to 6
- edit_in: float32 [73728], P(('parts', 'mp')), parts along dimension 0, may hold values from -0.03125 to 0.03125
- edit_out: float32 [9216], P(('parts', 'mp')), parts along dimension 0, may hold values from -6 to 6
- norm_gain: float32 [4608], P('mp'), may hold values from 0.5 to 1.5
- head: bfloat16 [4608, 8192], P(None, ('vocab', 'mp', 'rep')), may hold values from -0.25 to 0.25
- token_ids: int32 [128], P('parts'), parts along dimension 0, may hold values from 0 to 8191
Outputs:
- penalty: float32 [128], P(('parts', 'vocab', 'rep')), parts along dimension 0
- grad_in: float32 [73728], P(('parts', 'mp')), parts along dimension 0
- grad_out: float32 [9216], P(('parts', 'mp')), parts along dimension 0
There are 2 independent parts, one for each index of `parts`. A program takes and returns all parts, laid end to end along the dimension named above; an argument that names none is the same for every part. Nothing has to cross between parts.
All inputs are finite; a program needn't handle non-finite values.
Results may differ from a plain program's by a relative error of at most 0.011.
Values may be sent and summed in bfloat16 or wider, within the bound.
No kernel may reach another device: no remote copies, remote signals or barrier semaphores. Data moves between devices by JAX's collectives and lax.ppermute only.
A program may use at most 64 MiB of HBM per device.

v0:
```python
import jax
import jax.numpy as jnp
from jax import lax
from jax.sharding import PartitionSpec as P

D = 4608
softcap = 30.0
epsilon = 1e-06


def local(resid_base, mlp_hidden, edit_in, edit_out, norm_gain, head, token_ids):
    tok_rows = resid_base.shape[0]
    feat_cols = resid_base.shape[1]
    voc_cols = head.shape[1]
    hidden_f = mlp_hidden.astype(jnp.float32)
    base_f = resid_base.astype(jnp.float32)
    mix_part = jnp.sum(hidden_f * edit_in[None, :], axis=1)
    mix_scale, square_base, base_along, out_square = lax.psum(
        (
            mix_part,
            jnp.sum(base_f * base_f, axis=1),
            jnp.sum(base_f * edit_out[None, :], axis=1),
            jnp.sum(edit_out * edit_out),
        ),
        "mp",
    )
    resid = base_f + mix_scale[:, None] * edit_out[None, :]
    square_edit = square_base + 2.0 * mix_scale * base_along + mix_scale * mix_scale * out_square
    along = base_along + mix_scale * out_square
    edit_scale = lax.rsqrt(square_edit / D + epsilon)
    base_scale = lax.rsqrt(square_base / D + epsilon)
    x_edit = (resid * edit_scale[:, None] * norm_gain[None, :]).astype(jnp.bfloat16)
    x_base = (base_f * base_scale[:, None] * norm_gain[None, :]).astype(jnp.bfloat16)
    stacked = jnp.stack([x_edit, x_base], axis=0)
    direction = lax.all_gather(edit_out * norm_gain, "mp", axis=0, tiled=True)
    weights_all = lax.all_gather(mix_scale * edit_scale, ("vocab", "rep"), axis=0, tiled=True)
    full_cols = lax.all_gather(stacked, "mp", axis=2, tiled=True)
    logits_pre = jnp.einsum(
        "ktd,dv->ktv",
        lax.all_gather(full_cols, ("vocab", "rep"), axis=1, tiled=True),
        head,
        preferred_element_type=jnp.float32,
    )
    capped = softcap * jnp.tanh(logits_pre / softcap)
    totals = lax.psum(jnp.sum(jnp.exp(capped), axis=2), ("vocab", "mp", "rep"))
    log_totals = jnp.log(totals)
    probs = jnp.exp(capped - log_totals[:, :, None])
    z_edit = capped[0]
    z_base = capped[1]
    first_col = lax.axis_index(("vocab", "mp", "rep")) * voc_cols
    columns = first_col + jnp.arange(voc_cols, dtype=jnp.int32)
    onehot = (token_ids[:, None] == columns[None, :]).astype(jnp.float32)
    diff = z_base - z_edit
    kl_part = jnp.sum(probs[1] * diff, axis=1)
    gap_part = jnp.sum(onehot * diff, axis=1)
    dy_rows = ((2.0 * probs[0] - probs[1] - onehot) * (1.0 - (z_edit / softcap) ** 2)).astype(
        jnp.bfloat16
    )
    dx_part = lax.dot_general(
        dy_rows, head, (((1,), (1,)), ((), ())), preferred_element_type=jnp.float32
    )
    align_part = jnp.sum(logits_pre[0] * dy_rows.astype(jnp.float32), axis=1)
    proj_part = jnp.dot(dx_part, direction, precision=lax.Precision.HIGHEST)
    weighted_part = jnp.dot(weights_all, dx_part, precision=lax.Precision.HIGHEST)
    kl_all, gap_all, proj_all, align_all, weighted_all = lax.psum(
        (kl_part, gap_part, proj_part, align_part, weighted_part), ("vocab", "mp", "rep")
    )
    tok_start = lax.axis_index(("vocab", "rep")) * tok_rows
    feat_start = lax.axis_index("mp") * feat_cols
    kl_own = lax.dynamic_slice_in_dim(kl_all, tok_start, tok_rows, 0)
    gap_own = lax.dynamic_slice_in_dim(gap_all, tok_start, tok_rows, 0)
    proj_own = lax.dynamic_slice_in_dim(proj_all, tok_start, tok_rows, 0)
    align_own = lax.dynamic_slice_in_dim(align_all, tok_start, tok_rows, 0)
    lse_own = lax.dynamic_slice_in_dim(log_totals, tok_start, tok_rows, 1)
    penalty = kl_own + gap_own + 2.0 * (lse_own[0] - lse_own[1])
    normed = resid * edit_scale[:, None]
    shrink = edit_scale * align_own / D
    coeff = edit_scale * proj_own - shrink * (edit_scale * along)
    second_part = jnp.sum((mix_scale * shrink)[:, None] * normed, axis=0)
    grad_in_part = jnp.sum(coeff[:, None] * hidden_f, axis=0)
    second_sum, grad_in = lax.psum((second_part, grad_in_part), ("vocab", "rep"))
    weighted_own = lax.dynamic_slice_in_dim(weighted_all, feat_start, feat_cols, 0)
    grad_out = norm_gain * weighted_own - second_sum
    return (penalty, grad_in, grad_out)


def solution(mesh):
    in_specs = (
        P(("parts", "vocab", "rep"), "mp"),
        P(("parts", "vocab", "rep"), "mp"),
        P(("parts", "mp")),
        P(("parts", "mp")),
        P("mp"),
        P(None, ("vocab", "mp", "rep")),
        P("parts"),
    )
    out_specs = (P(("parts", "vocab", "rep")), P(("parts", "mp")), P(("parts", "mp")))
    return jax.shard_map(local, mesh=mesh, in_specs=in_specs, out_specs=out_specs, check_vma=False)
```

profile of v0, /device:TPU:8, one launch (start us, length us, event | category | flops | bytes accessed | tf_op | source)
XLA Modules:
  0.0 234.1 jit_solution(15880379331970252911)
XLA Ops:
  7.2 0.0 all-gather.3.cloned.1.call-start
  7.2 1.3 fusion.23
  8.6 0.9 fusion.15
  9.5 1.2 fusion.2
  10.7 1.2 dynamic-slice
  12.6 5.6 %all-reduce.2 = (f32[8]{0:T(128)S(1)}, f32[8]{0:T(128)S(1)}, f32[8]{0:T(128)S(1)}, f32[]{:T(128)}) all-reduce(f32[8]{0:T(128)S(1)} %get-tuple-element.6, f32[8]{0:T(128)S(1)} %fusion.2, f32[8]{0:T(128)S(1)} %get-tuple-element.5, f32[]{:T(128)} %get-tuple-element.26), channel_id=1, replica_groups=mesh['parts'=2,'vocab'=4,'mp'=2,'rep'=2] {'mp'}, use_global_device_ids=true, to_apply=%region_3.0 | all-reduce | flops 25 | bytes 200 | tf_op jit(solution)/shard_map/psum | solution.py:18
  18.2 0.7 multiply_dynamic-update-slice_fusion
  19.0 0.9 fusion.18
  19.9 5.1 %all_gather.12 = bf16[2,8,4608]{2,1,0:T(8,128)(2,1)} all-gather(bf16[2,8,2304]{2,1,0:T(8,128)(2,1)S(1)} %pad_maximum_fusion), channel_id=1, replica_groups=mesh['parts'=2,'vocab'=4,'mp'=2,'rep'=2] {'mp'}, dimensions={2}, use_global_device_ids=true | all-gather | bytes 221184 | tf_op jit(solution)/shard_map/all_gather | solution.py:37
  25.0 0.0 all-gather.3.cloned.1.call-update
  25.0 0.0 all-reduce.5.cloned.1.call-start
  25.1 10.7 %all-reduce = f32[64]{0:T(128)S(1)} all-reduce(f32[64]{0:T(128)S(1)} %get-tuple-element.15), channel_id=1, replica_groups=mesh['parts'=2,'vocab'=4,'mp'=2,'rep'=2] {'vocab','rep'}, use_global_device_ids=true, to_apply=%add | all-reduce | flops 64 | bytes 512
  35.8 4.4 %all-gather = f32[2,1,2304]{2,1,0:T(1,128)S(1)} all-gather(f32[1,1,2304]{2,1,0:T(1,128)S(1)} %reshape.34), channel_id=1, replica_groups=mesh['parts'=2,'vocab'=4,'mp'=2,'rep'=2] {'mp'}, dimensions={0}, use_global_device_ids=true | all-gather | bytes 27648 | tf_op jit(solution)/shard_map/all_gather | solution.py:35
  40.2 0.0 copy-start.4
  40.2 9.0 %all-gather.3.cloned.1.call-done = bf16[2,64,4608]{2,1,0:T(8,128)(2,1)} async-done(((bf16[2,8,4608]{2,1,0:T(8,128)(2,1)}), bf16[2,64,4608]{2,1,0:T(8,128)(2,1)}) %all-gather.3.cloned.1.call-update) | async-done | bytes 1179664 | tf_op jit(solution)/shard_map/all_gather | solution.py:40
  49.2 3.6 %exponential_reduce_fusion = (f32[2,64]{1,0:T(2,128)S(1)}, f32[2,64,512]{2,1,0:T(8,128)S(1)}) fusion(bf16[2,64,4608]{2,1,0:T(8,128)(2,1)} %all-gather.3.cloned.1.call-done, bf16[4608,512]{1,0:T(8,128)(2,1)} %param.12), kind=kOutput, calls=%fused_computation.9 | convolution fusion | flops 604176256 | bytes 6160896 | tf_op jit(solution)/shard_map/ktd,dv->ktv/dot_general | solution.py:38
  52.8 24.3 %psum.88 = f32[2,64]{1,0:T(2,128)S(1)} all-reduce(f32[2,64]{1,0:T(2,128)S(1)} %get-tuple-element.30), channel_id=1, replica_groups=mesh['parts'=2,'vocab'=4,'mp'=2,'rep'=2] {'vocab','mp','rep'}, use_global_device_ids=true, to_apply=%region_9.0 | all-reduce | flops 128 | bytes 1024 | tf_op jit(solution)/shard_map/psum | solution.py:45
  77.1 0.1 subtract_exponential_fusion
  77.2 0.0 copy-done.4
  77.2 0.2 fusion.9
  77.4 3.9 %fusion.24 = f32[64,4608]{1,0:T(8,128)S(1)} fusion(bf16[64,512]{1,0:T(8,128)(2,1)S(1)} %get-tuple-element.18, bf16[4608,512]{1,0:T(8,128)(2,1)} %param.12), kind=kOutput, calls=%fused_computation.54 | convolution fusion | flops 301989888 | bytes 5963776 | tf_op jit(solution)/shard_map/dot_general | solution.py:59
  81.3 0.0 copy-start.1
  81.3 0.0 copy-start.2
  81.3 0.0 copy-start
  81.3 0.7 convolution_reduce_fusion
  82.0 0.0 copy-start.3
  82.0 1.0 convolution_bitcast_fusion
  83.1 0.1 constant_dynamic-slice_fusion
  83.1 57.7 %all-reduce.1 = (f32[64]{0:T(128)S(1)}, f32[64]{0:T(128)S(1)}, f32[64]{0:T(128)S(1)}, f32[4608]{0:T(1024)S(1)}) all-reduce(f32[64]{0:T(128)S(1)} %add.92, f32[64]{0:T(128)S(1)} %convolution_bitcast_fusion, f32[64]{0:T(128)S(1)} %get-tuple-element.17, ...), channel_id=1, replica_groups=mesh['parts'=2,'vocab'=4,'mp'=2,'rep'=2] {'vocab','mp','rep'}, use_global_device_ids=true, to_apply=%region_11.0 | all-reduce | flops 4800 | bytes 38400 | tf_op jit(solution)/shard_map/psum | solution.py:65
  140.8 0.7 fusion.21
  141.5 0.0 copy-done.1
  141.5 0.0 copy-done.2
  141.5 0.1 multiply_reduce_fusion.1
  141.6 30.3 %psum.95 = f32[2304]{0:T(1024)S(1)} all-reduce(f32[2304]{0:T(1024)S(1)} %multiply_reduce_fusion.1), channel_id=1, replica_groups=mesh['parts'=2,'vocab'=4,'mp'=2,'rep'=2] {'vocab','rep'}, use_global_device_ids=true, to_apply=%region_21.0 | all-reduce | flops 2304 | bytes 18432 | tf_op jit(solution)/shard_map/psum | solution.py:81
  171.9 0.0 copy-done
  171.9 1.0 fusion.3
  172.9 0.0 all-reduce.5.cloned.1.call-update
  172.9 0.0 copy-done.3
  173.0 0.7 multiply_subtract_fusion
  173.6 0.6 bitcast_add_fusion
  174.2 51.5 %all-reduce.5.cloned.1.call-done = f32[18432]{0:T(1024)} async-done(((f32[18432]{0:T(1024)}), f32[18432]{0:T(1024)}) %all-reduce.5.cloned.1.call-update) | async-done | bytes 73744 | tf_op jit(solution)/shard_map/psum | solution.py:81
  225.7 1.5 copy.12
  (6 shorter events, 0.0 us)
Async XLA Ops:
  7.2 42.0 %all-gather.3.cloned.1.call-start = ((), (), s32[]{:S(2)}) async-start(), calls=%async_computation | async-start | bytes 1327104 | tf_op jit(solution)/shard_map/all_gather | solution.py:40
  25.0 200.7 %all-reduce.5.cloned.1.call-start = ((), (), s32[]{:S(2)}) async-start(), calls=%async_computation.1 | async-start | bytes 147456 | tf_op jit(solution)/shard_map/psum | solution.py:81
  40.2 37.0 %copy-start.4 = (s32[64]{0:T(128)S(1)}, s32[64]{0:T(128)}, u32[]{:S(2)}) copy-start(s32[64]{0:T(128)} %param.13) | copy-start | bytes 772
  81.3 60.2 %copy-start.1 = (bf16[8,2304]{1,0:T(8,128)(2,1)S(1)}, bf16[8,2304]{1,0:T(8,128)(2,1)}, u32[]{:S(2)}) copy-start(bf16[8,2304]{1,0:T(8,128)(2,1)} %param.7) | copy-start | bytes 110596
  81.3 60.2 %copy-start.2 = (f32[2304]{0:T(1024)S(1)}, f32[2304]{0:T(1024)}, u32[]{:S(2)}) copy-start(f32[2304]{0:T(1024)} %param.10) | copy-start | bytes 27652
  81.3 90.6 %copy-start = (bf16[8,18432]{1,0:T(8,128)(2,1)S(1)}, bf16[8,18432]{1,0:T(8,128)(2,1)}, u32[]{:S(2)}) copy-start(bf16[8,18432]{1,0:T(8,128)(2,1)} %param.8) | copy-start | bytes 884740
  82.0 90.9 %copy-start.3 = (f32[2304]{0:T(1024)S(1)}, f32[2304]{0:T(1024)}, u32[]{:S(2)}) copy-start(f32[2304]{0:T(1024)} %param.11) | copy-start | bytes 27652
Sparse Core Ops, SparseCore 0:
  25.1 24.0 all-gather.2
  173.1 52.6 all-reduce.4
where the time goes:
time: 235 us; the launch traced here: 234 us
  blocking collectives  138 us (59%)
  waiting for transfers between devices  60.5 us (26%)
  between operations  14.8 us (6%)
  matrix products  9.18 us (4%)
  other arithmetic  8.58 us (4%)
  local copies, waits for them, and re-layouts  2.88 us (1%)
    psum x1, blocking collectives, local(): lax.psum((kl_part, gap_part, proj_part, align_part, weighted_part), ('voc...  57.7 us
    psum x1, waiting for transfers between devices, local(): lax.psum((second_part, grad_in_part), ('vocab', 'rep'))  51.5 us
    psum x1, blocking collectives, local(): lax.psum((second_part, grad_in_part), ('vocab', 'rep'))  30.3 us
    psum x1, blocking collectives, local(): totals = lax.psum(jnp.sum(jnp.exp(capped), axis=2), ('vocab', 'mp', 'rep'))  24.3 us
    unnamed x1, blocking collectives  10.7 us
    all_gather x1, waiting for transfers between devices, local(): lax.all_gather(full_cols, ('vocab', 'rep'), axis=1, tiled=True)  9 us
    psum x1, blocking collectives, local(): lax.psum((mix_part, jnp.sum(base_f * base_f, axis=1), jnp.sum(base_f * ed...  5.58 us
    all_gather x1, blocking collectives, local(): full_cols = lax.all_gather(stacked, 'mp', axis=2, tiled=True)  5.14 us
  transfers between devices with their start and end apart: 2, of which 2 were waited for; matrix products, arithmetic and copies ran while one was open for 1% of the time, Pallas kernels for 0%

commit v1 on v0

--- a/solution.py
+++ b/solution.py
@@ -42,7 +42,9 @@
         preferred_element_type=jnp.float32,
     )
     capped = softcap * jnp.tanh(logits_pre / softcap)
-    totals = lax.psum(jnp.sum(jnp.exp(capped), axis=2), ("vocab", "mp", "rep"))
+    totals = jnp.sum(
+        lax.all_gather(jnp.sum(jnp.exp(capped), axis=2), ("vocab", "mp", "rep")), axis=0
+    )
     log_totals = jnp.log(totals)
     probs = jnp.exp(capped - log_totals[:, :, None])
     z_edit = capped[0]

time: 235 us -> 223 us (0.949)
  blocking collectives: 138 us -> 126 us
    psum x1 -> x0, blocking collectives: 24.3 us -> none  [local(): totals = lax.psum(jnp.sum(jnp.exp(capped), axis=2), ('vocab', 'mp', 'rep'))]
    all_gather x0 -> x1, blocking collectives: none -> 17.2 us  [local(): lax.all_gather(jnp.sum(jnp.exp(capped), axis=2), ('vocab', 'mp', 'rep'))]
    psum x1, blocking collectives: 57.7 us -> 52.6 us  [local(): lax.psum((kl_part, gap_part, proj_part, align_part, weighted_part), ('voc...]
where the time goes in v1:
time: 223 us; the launch traced here: 222 us
  blocking collectives  126 us (57%)
  waiting for transfers between devices  60.5 us (27%)
  between operations  14.8 us (7%)
  matrix products  9.18 us (4%)
  other arithmetic  8.6 us (4%)
  local copies, waits for them, and re-layouts  2.88 us (1%)
    psum x1, blocking collectives, local(): lax.psum((kl_part, gap_part, proj_part, align_part, weighted_part), ('voc...  52.6 us
    psum x1, waiting for transfers between devices, local(): lax.psum((second_part, grad_in_part), ('vocab', 'rep'))  51.5 us
    psum x1, blocking collectives, local(): lax.psum((second_part, grad_in_part), ('vocab', 'rep'))  30.3 us
    all_gather x1, blocking collectives, local(): lax.all_gather(jnp.sum(jnp.exp(capped), axis=2), ('vocab', 'mp', 'rep'))  17.2 us
    unnamed x1, blocking collectives  10.7 us
    all_gather x1, waiting for transfers between devices, local(): lax.all_gather(full_cols, ('vocab', 'rep'), axis=1, tiled=True)  9 us
    psum x1, blocking collectives, local(): lax.psum((mix_part, jnp.sum(base_f * base_f, axis=1), jnp.sum(base_f * ed...  5.58 us
    all_gather x1, blocking collectives, local(): full_cols = lax.all_gather(stacked, 'mp', axis=2, tiled=True)  5.14 us
  transfers between devices with their start and end apart: 2, of which 2 were waited for; matrix products, arithmetic and copies ran while one was open for 1% of the time, Pallas kernels for 0%

profile of v1, /device:TPU:8, one launch (start us, length us, event | category | flops | bytes accessed | tf_op | source)
XLA Modules:
  0.0 222.0 jit_solution(4937958762853988680)
XLA Ops:
  7.2 0.0 all-gather.5.cloned.1.call-start
  7.2 1.3 fusion.23
  8.6 0.9 fusion.15
  9.5 1.2 fusion.2
  10.7 1.2 dynamic-slice
  12.6 5.6 %all-reduce.2 = (f32[8]{0:T(128)S(1)}, f32[8]{0:T(128)S(1)}, f32[8]{0:T(128)S(1)}, f32[]{:T(128)}) all-reduce(f32[8]{0:T(128)S(1)} %get-tuple-element.6, f32[8]{0:T(128)S(1)} %fusion.2, f32[8]{0:T(128)S(1)} %get-tuple-element.5, f32[]{:T(128)} %get-tuple-element.26), channel_id=1, replica_groups=mesh['parts'=2,'vocab'=4,'mp'=2,'rep'=2] {'mp'}, use_global_device_ids=true, to_apply=%region_3.0 | all-reduce | flops 25 | bytes 200 | tf_op jit(solution)/shard_map/psum | solution.py:18
  18.2 0.7 multiply_dynamic-update-slice_fusion
  19.0 0.9 fusion.18
  19.9 5.1 %all_gather.18 = bf16[2,8,4608]{2,1,0:T(8,128)(2,1)} all-gather(bf16[2,8,2304]{2,1,0:T(8,128)(2,1)S(1)} %pad_maximum_fusion), channel_id=1, replica_groups=mesh['parts'=2,'vocab'=4,'mp'=2,'rep'=2] {'mp'}, dimensions={2}, use_global_device_ids=true | all-gather | bytes 221184 | tf_op jit(solution)/shard_map/all_gather | solution.py:37
  25.0 0.0 all-gather.5.cloned.1.call-update
  25.0 0.0 all-reduce.5.cloned.1.call-start
  25.1 10.7 %all-reduce = f32[64]{0:T(128)S(1)} all-reduce(f32[64]{0:T(128)S(1)} %get-tuple-element.15), channel_id=1, replica_groups=mesh['parts'=2,'vocab'=4,'mp'=2,'rep'=2] {'vocab','rep'}, use_global_device_ids=true, to_apply=%add | all-reduce | flops 64 | bytes 512
  35.8 4.4 %all-gather.2 = f32[2,1,2304]{2,1,0:T(1,128)S(1)} all-gather(f32[1,1,2304]{2,1,0:T(1,128)S(1)} %reshape.39), channel_id=1, replica_groups=mesh['parts'=2,'vocab'=4,'mp'=2,'rep'=2] {'mp'}, dimensions={0}, use_global_device_ids=true | all-gather | bytes 27648 | tf_op jit(solution)/shard_map/all_gather | solution.py:35
  40.2 0.0 copy-start.4
  40.2 9.0 %all-gather.5.cloned.1.call-done = bf16[2,64,4608]{2,1,0:T(8,128)(2,1)} async-done(((bf16[2,8,4608]{2,1,0:T(8,128)(2,1)}), bf16[2,64,4608]{2,1,0:T(8,128)(2,1)}) %all-gather.5.cloned.1.call-update) | async-done | bytes 1179664 | tf_op jit(solution)/shard_map/all_gather | solution.py:40
  49.2 3.6 %exponential_reduce_fusion = (f32[2,64]{1,0:T(2,128)S(1)}, f32[2,64,512]{2,1,0:T(8,128)S(1)}) fusion(bf16[2,64,4608]{2,1,0:T(8,128)(2,1)} %all-gather.5.cloned.1.call-done, bf16[4608,512]{1,0:T(8,128)(2,1)} %param.12), kind=kOutput, calls=%fused_computation.9 | convolution fusion | flops 604176256 | bytes 6160896 | tf_op jit(solution)/shard_map/ktd,dv->ktv/dot_general | solution.py:38
  52.8 17.2 %all-gather.1 = f32[16,2,64]{2,1,0:T(2,128)S(1)} all-gather(f32[1,2,64]{2,1,0:T(2,128)S(1)} %bitcast.55), channel_id=2, replica_groups=mesh['parts'=2,'vocab'=4,'mp'=2,'rep'=2] {'vocab','mp','rep'}, dimensions={0}, use_global_device_ids=true | all-gather | bytes 8704 | tf_op jit(solution)/shard_map/all_gather | solution.py:46
  70.1 0.1 subtract_exponential_fusion
  70.2 0.0 copy-done.4
  70.2 0.2 fusion.9
  70.4 3.9 %fusion.24 = f32[64,4608]{1,0:T(8,128)S(1)} fusion(bf16[64,512]{1,0:T(8,128)(2,1)S(1)} %get-tuple-element.18, bf16[4608,512]{1,0:T(8,128)(2,1)} %param.12), kind=kOutput, calls=%fused_computation.54 | convolution fusion | flops 301989888 | bytes 5963776 | tf_op jit(solution)/shard_map/dot_general | solution.py:61
  74.3 0.0 copy-start.1
  74.3 0.0 copy-start.2
  74.3 0.0 copy-start
  74.3 0.7 convolution_reduce_fusion
  75.0 0.0 copy-start.3
  75.0 1.0 convolution_bitcast_fusion
  76.1 0.1 constant_dynamic-slice_fusion
  76.1 52.6 %all-reduce.1 = (f32[64]{0:T(128)S(1)}, f32[64]{0:T(128)S(1)}, f32[64]{0:T(128)S(1)}, f32[4608]{0:T(1024)S(1)}) all-reduce(f32[64]{0:T(128)S(1)} %add.90, f32[64]{0:T(128)S(1)} %convolution_bitcast_fusion, f32[64]{0:T(128)S(1)} %get-tuple-element.17, ...), channel_id=1, replica_groups=mesh['parts'=2,'vocab'=4,'mp'=2,'rep'=2] {'vocab','mp','rep'}, use_global_device_ids=true, to_apply=%region_11.0 | all-reduce | flops 4800 | bytes 38400 | tf_op jit(solution)/shard_map/psum | solution.py:67
  128.8 0.7 fusion.21
  129.5 0.0 copy-done.1
  129.5 0.0 copy-done.2
  129.5 0.1 multiply_reduce_fusion.1
  129.6 30.3 %psum.87 = f32[2304]{0:T(1024)S(1)} all-reduce(f32[2304]{0:T(1024)S(1)} %multiply_reduce_fusion.1), channel_id=1, replica_groups=mesh['parts'=2,'vocab'=4,'mp'=2,'rep'=2] {'vocab','rep'}, use_global_device_ids=true, to_apply=%region_21.0 | all-reduce | flops 2304 | bytes 18432 | tf_op jit(solution)/shard_map/psum | solution.py:83
  159.9 0.0 copy-done
  159.9 1.0 fusion.3
  160.9 0.0 all-reduce.5.cloned.1.call-update
  160.9 0.0 copy-done.3
  160.9 0.7 multiply_subtract_fusion
  161.6 0.6 bitcast_add_fusion
  162.2 51.5 %all-reduce.5.cloned.1.call-done = f32[18432]{0:T(1024)} async-done(((f32[18432]{0:T(1024)}), f32[18432]{0:T(1024)}) %all-reduce.5.cloned.1.call-update) | async-done | bytes 73744 | tf_op jit(solution)/shard_map/psum | solution.py:83
  213.7 1.5 copy.12
  (7 shorter events, 0.1 us)
Async XLA Ops:
  7.2 42.0 %all-gather.5.cloned.1.call-start = ((), (), s32[]{:S(2)}) async-start(), calls=%async_computation | async-start | bytes 1327104 | tf_op jit(solution)/shard_map/all_gather | solution.py:40
  25.0 188.7 %all-reduce.5.cloned.1.call-start = ((), (), s32[]{:S(2)}) async-start(), calls=%async_computation.1 | async-start | bytes 147456 | tf_op jit(solution)/shard_map/psum | solution.py:83
  40.2 30.0 %copy-start.4 = (s32[64]{0:T(128)S(1)}, s32[64]{0:T(128)}, u32[]{:S(2)}) copy-start(s32[64]{0:T(128)} %param.13) | copy-start | bytes 772
  74.3 55.2 %copy-start.1 = (bf16[8,2304]{1,0:T(8,128)(2,1)S(1)}, bf16[8,2304]{1,0:T(8,128)(2,1)}, u32[]{:S(2)}) copy-start(bf16[8,2304]{1,0:T(8,128)(2,1)} %param.7) | copy-start | bytes 110596
  74.3 55.2 %copy-start.2 = (f32[2304]{0:T(1024)S(1)}, f32[2304]{0:T(1024)}, u32[]{:S(2)}) copy-start(f32[2304]{0:T(1024)} %param.10) | copy-start | bytes 27652
  74.3 85.6 %copy-start = (bf16[8,18432]{1,0:T(8,128)(2,1)S(1)}, bf16[8,18432]{1,0:T(8,128)(2,1)}, u32[]{:S(2)}) copy-start(bf16[8,18432]{1,0:T(8,128)(2,1)} %param.8) | copy-start | bytes 884740
  75.0 85.9 %copy-start.3 = (f32[2304]{0:T(1024)S(1)}, f32[2304]{0:T(1024)}, u32[]{:S(2)}) copy-start(f32[2304]{0:T(1024)} %param.11) | copy-start | bytes 27652
Sparse Core Ops, SparseCore 0:
  25.1 24.0 all-gather.4
  161.0 52.6 all-reduce.4
